TPU v7x, 32 devices: a whole 2x2x4 slice. The times are simulated.
32 devices in a mesh: group: 4 (over y, core), member: 8 (over z, x).
Axes of the slice: x: 2, y: 2, z: 4, core: 2. Of those that a mesh axis runs over, the one named last changes fastest.
Arguments:
- leaf_solution: bfloat16 [256, 64, 128], P(('group', 'member')), may hold values from -6 to 6
- leaf_panels: bfloat16 [256, 3, 4, 128, 128], P(('group', 'member')), may hold values from -0.09375 to 0.09375
- leaf_rows: int32 [256, 3, 4], P(('group', 'member')), may hold values from 0 to 31, as said below
- sep_panels: bfloat16 [32, 3, 4, 128, 128], P(('group', 'member')), may hold values from -0.25 to 0.25
- sep_rows: int32 [32, 3, 4], P(('group', 'member')), may hold values from 0 to 31, as said below
- right_sides: bfloat16 [3, 32, 64, 128], P(None, ('group', 'member')), may hold values from -6 to 6
- inverse_low: bfloat16 [32, 1024, 128], P(('group', 'member')), may hold values from -0.1875 to 0.1875
- inverse_mid: bfloat16 [32, 2048, 128], P(('group', 'member')), may hold values from -0.125 to 0.125
- inverse_top: bfloat16 [32, 4096, 128], P(('group', 'member')), may hold values from -0.09375 to 0.09375
Outputs:
- solution: bfloat16 [3, 32, 64, 128], P(None, ('group', 'member'))
Inputs may be any that keep to these rules, and one draw needn't show every extreme that they name: leaf_rows[k, l, t] is below 8 * 2**l: a block of the ancestor separator at level l; indices may repeat. sep_rows[d, j, t] is below 16, 32, 32 for j = 0, 1, 2: a block of the target separator; indices may repeat.
All inputs are finite; a program needn't handle non-finite values.
Results may differ from a plain program's by a relative error of at most 0.012.
Values may be sent and summed in bfloat16 or wider, within the bound.
A program may use at most 128 MiB of HBM per device.

v0:
```python
import jax
import jax.numpy as jnp
from jax import lax
from jax.sharding import PartitionSpec as P


def swapped(value, axis, stride):
    mask = 2**stride
    pairs = [(source, source ^ mask) for source in range(lax.axis_size(axis))]
    return lax.ppermute(value, axis, pairs)


def spread(terms, rows, blocks):
    count = terms.shape[0]
    onehot = (rows[:, None] == jnp.arange(blocks, dtype=jnp.int32)[None, :]).astype(jnp.float32)
    flat = lax.dot_general(
        onehot, terms.reshape(count, -1), (((0,), (0,)), ((), ())), precision=lax.Precision.HIGHEST
    )
    return flat.reshape(blocks, terms.shape[1], terms.shape[2])


def collect(buffer, level, group_index):
    count = 2**level
    members = buffer.shape[0] // count
    height, width = (buffer.shape[1], buffer.shape[2])
    parts = lax.psum_scatter(
        buffer.reshape(count, members, height, width), "member", scatter_dimension=1, tiled=True
    )
    parts = parts.reshape(count, height, width)
    if level == 0:
        return parts[0]
    for bit in reversed(range(level)):
        halves = parts.reshape(2, -1, height, width)
        upper = group_index >> bit & 1
        keep = jnp.where(upper == 1, halves[1], halves[0])
        outgoing = jnp.where(upper == 1, halves[0], halves[1])
        parts = keep + swapped(outgoing, "group", bit)
    return parts[0]


def settle(resid, inverse, level, group_index):
    whole = lax.all_gather(resid, "member", axis=1, tiled=True)
    if level == 0:
        return jnp.dot(whole, inverse, preferred_element_type=jnp.float32).astype(jnp.bfloat16)
    count = 2**level
    width = whole.shape[1]
    held = whole[None]
    for bit in range(level):
        other = swapped(held, "group", bit)
        upper = group_index >> bit & 1
        held = jnp.where(
            upper == 1, jnp.concatenate([other, held], 0), jnp.concatenate([held, other], 0)
        )
    shaped = inverse.reshape(count, width, inverse.shape[1])
    total = jnp.einsum("qrk,qkp->rp", held, shaped, preferred_element_type=jnp.float32)
    return total.astype(jnp.bfloat16)


def on_device(
    leaf_solution,
    leaf_panels,
    leaf_rows,
    sep_panels,
    sep_rows,
    right_sides,
    inverse_low,
    inverse_mid,
    inverse_top,
):
    group_index = lax.axis_index("group")
    members = lax.axis_size("member")
    height, width = (leaf_solution.shape[1], leaf_solution.shape[2])
    terms = jnp.einsum(
        "brp,bltpq->bltrq", leaf_solution, leaf_panels, preferred_element_type=jnp.float32
    )
    leaf_parts = [
        spread(
            terms[:, level].reshape(-1, height, width),
            leaf_rows[:, level].reshape(-1),
            members * 2**level,
        )
        for level in range(3)
    ]
    base_mid = leaf_parts[1]
    base_top = leaf_parts[2]
    resid = (right_sides[0, 0].astype(jnp.float32) - collect(leaf_parts[0], 0, group_index)).astype(
        jnp.bfloat16
    )
    first = settle(resid, inverse_low[0], 0, group_index)
    upward = jnp.einsum(
        "rp,ktpq->ktrq", first, sep_panels[0, :2], preferred_element_type=jnp.float32
    )
    buffer_mid = base_mid + spread(upward[0], sep_rows[0, 0], members * 2)
    resid = (right_sides[1, 0].astype(jnp.float32) - collect(buffer_mid, 1, group_index)).astype(
        jnp.bfloat16
    )
    second = settle(resid, inverse_mid[0], 1, group_index)
    onward = jnp.einsum("rp,tpq->trq", second, sep_panels[0, 2], preferred_element_type=jnp.float32)
    sources = jnp.concatenate([upward[1], onward], 0)
    targets = jnp.concatenate([sep_rows[0, 1], sep_rows[0, 2]], 0)
    buffer_top = base_top + spread(sources, targets, members * 4)
    resid = (right_sides[2, 0].astype(jnp.float32) - collect(buffer_top, 2, group_index)).astype(
        jnp.bfloat16
    )
    third = settle(resid, inverse_top[0], 2, group_index)
    return jnp.stack([first, second, third])[:, None]


def solution(mesh):
    placed = (
        P(("group", "member"), None, None),
        P(("group", "member"), None, None, None, None),
        P(("group", "member"), None, None),
        P(("group", "member"), None, None, None, None),
        P(("group", "member"), None, None),
        P(None, ("group", "member"), None, None),
        P(("group", "member"), None, None),
        P(("group", "member"), None, None),
        P(("group", "member"), None, None),
    )
    return jax.shard_map(
        on_device,
        mesh=mesh,
        in_specs=placed,
        out_specs=P(None, ("group", "member"), None, None),
        check_vma=False,
    )
```

profile of v0, /device:TPU:0, one launch (start us, length us, event | category | flops | bytes accessed | tf_op | source)
XLA Modules:
  0.0 334.2 jit_solution(11775017995202227843)
XLA Ops:
  6.5 0.0 copy-start
  6.5 0.0 reduce-scatter.6.cloned.1.call-start
  6.5 1.9 copy-done
  8.4 1.5 convolution_bitcast_fusion
  9.9 0.0 copy-start.3
  9.9 0.0 copy-start.4
  9.9 1.7 fusion.58
  11.7 0.0 copy-done.3
  11.7 0.6 fusion.59
  12.2 0.1 copy.27
  12.3 0.1 eq.42
  12.4 2.2 convolution_bitcast_fusion.1
  14.6 0.8 copy.29
  15.4 0.0 reduce-scatter.6.cloned.1.call-update
  15.4 0.0 all-reduce.3.cloned.1.call-start
  15.5 0.1 copy.31
  15.5 0.1 eq.91
  15.6 0.0 copy-done.4
  15.6 0.6 slice_bitcast_fusion.3
  16.2 3.0 fusion.8
  19.3 61.1 %reduce-scatter.6.cloned.1.call-done = f32[1,1,64,128]{3,2,0,1:T(8,128)} async-done(((f32[1,8,64,128]{3,2,0,1:T(8,128)}), f32[1,1,64,128]{3,2,0,1:T(8,128)}) %reduce-scatter.6.cloned.1.call-update) | async-done | bytes 32784 | tf_op jit(solution)/shard_map/reduce_scatter | solution.py:26
  80.3 0.8 fusion.37
  81.1 26.1 %all-gather = bf16[1,1,64,1024]{3,2,1,0:T(8,128)(2,1)S(1)} all-gather(bf16[1,1,64,128]{3,2,1,0:T(8,128)(2,1)S(1)} %fusion.37), channel_id=2, replica_groups=mesh['group'=4,'member'=8] {'member'}, dimensions={3}, use_global_device_ids=true | all-gather | bytes 147456 | tf_op jit(solution)/shard_map/all_gather | solution.py:42
  107.2 1.1 convolution_convert_fusion
  108.4 0.2 convolution_bitcast_fusion.2
  108.5 0.0 copy-start.2
  108.6 1.6 fusion.1
  110.2 1.0 copy.33
  111.1 0.0 all-reduce.3.cloned.1.call-update
  111.2 0.0 reduce-scatter.8.cloned.1.call-start
  111.2 1.2 dynamic-slice
  112.5 69.0 %all-reduce.3.cloned.1.call-done = f32[2,8,64,128]{3,2,1,0:T(8,128)} async-done(((f32[2,8,64,128]{3,2,1,0:T(8,128)}), f32[2,8,64,128]{3,2,1,0:T(8,128)}) %all-reduce.3.cloned.1.call-update) | async-done | bytes 524304
  181.5 1.3 select_bitcast_fusion.1
  182.8 0.0 collective-permute-start
  182.8 0.8 copy.34
  183.6 0.6 eq.100
  184.1 0.0 collective-permute-done
  184.2 1.3 fusion.36
  185.5 26.1 %all_gather.10 = bf16[64,1024]{1,0:T(8,128)(2,1)S(1)} all-gather(bf16[64,128]{1,0:T(8,128)(2,1)S(1)} %fusion.36), channel_id=1, replica_groups=mesh['group'=4,'member'=8] {'member'}, dimensions={1}, use_global_device_ids=true | all-gather | bytes 147456 | tf_op jit(solution)/shard_map/all_gather | solution.py:42
  211.6 0.0 collective-permute-start.1
  211.6 2.5 fusion.5
  214.1 0.8 pad_add_fusion
  214.9 0.1 copy.79
  215.0 0.0 collective-permute-done.1
  215.0 1.3 fusion.2
  216.3 1.1 convolution_bitcast_fusion.3
  217.3 0.1 copy.78
  217.4 0.7 fusion
  218.1 1.6 copy.36
  219.7 0.0 reduce-scatter.8.cloned.1.call-update
  219.8 62.2 %reduce-scatter.8.cloned.1.call-done = f32[4,1,64,128]{3,2,0,1:T(8,128)} async-done(((f32[4,8,64,128]{3,2,0,1:T(8,128)}), f32[4,1,64,128]{3,2,0,1:T(8,128)}) %reduce-scatter.8.cloned.1.call-update) | async-done | bytes 131088 | tf_op jit(solution)/shard_map/reduce_scatter | solution.py:26
  282.0 0.9 select_bitcast_fusion
  282.9 1.5 collective-permute-start.2
  284.4 2.8 collective-permute-done.2
  287.2 0.9 bitcast_add_fusion
  288.1 0.1 collective-permute-start.3
  288.2 1.2 collective-permute-done.3
  289.4 26.2 %all_gather.11 = bf16[64,1024]{1,0:T(8,128)(2,1)S(1)} all-gather(bf16[64,128]{1,0:T(8,128)(2,1)S(1)} %fusion.35), channel_id=1, replica_groups=mesh['group'=4,'member'=8] {'member'}, dimensions={1}, use_global_device_ids=true | all-gather | bytes 147456 | tf_op jit(solution)/shard_map/all_gather | solution.py:42
  315.6 0.0 collective-permute-start.4
  315.6 1.3 collective-permute-done.4
  317.0 1.5 collective-permute-start.5
  318.5 6.9 %collective-permute-done.5 = bf16[2,64,1024]{2,1,0:T(8,128)(2,1)S(1)} collective-permute-done((bf16[2,64,1024]{2,1,0:T(8,128)(2,1)S(1)}, bf16[2,64,1024]{2,1,0:T(8,128)(2,1)S(1)}, u32[]{:S(2)}, u32[]{:S(2)}) %collective-permute-start.5) | collective-permute-done | bytes 262176 | tf_op jit(solution)/shard_map/ppermute | solution.py:10
  325.4 1.6 fusion.4
  327.0 0.6 maximum_bitcast_fusion.2
  (7 shorter events, 0.1 us)
Async XLA Ops:
  6.5 1.9 copy-start
  6.5 73.8 %reduce-scatter.6.cloned.1.call-start = ((), (), s32[]{:S(2)}) async-start(), calls=%async_computation.2 | async-start | bytes 294912 | tf_op jit(solution)/shard_map/reduce_scatter | solution.py:26
  9.9 1.8 copy-start.3
  9.9 5.7 %copy-start.4 = (s32[1,3,4]{2,0,1:T(1,128)S(1)}, s32[1,3,4]{2,0,1:T(1,128)}, u32[]{:S(2)}) copy-start(s32[1,3,4]{2,0,1:T(1,128)} %param.13) | copy-start | bytes 148
  11.7 96.7 %copy-start.1 = (bf16[1,3,4,128,128]{4,3,2,1,0:T(8,128)(2,1)S(1)}, bf16[1,3,4,128,128]{4,3,2,1,0:T(8,128)(2,1)}, u32[]{:S(2)}) copy-start(bf16[1,3,4,128,128]{4,3,2,1,0:T(8,128)(2,1)} %param.12) | copy-start | bytes 1179652
  15.4 166.0 %all-reduce.3.cloned.1.call-start = ((), (), s32[]{:S(2)}) async-start(), calls=%async_computation.4 | async-start | bytes 1048576
  108.5 75.6 %copy-start.2 = (bf16[3,1,64,128]{3,2,1,0:T(8,128)(2,1)S(1)}, bf16[3,1,64,128]{3,2,1,0:T(8,128)(2,1)}, u32[]{:S(2)}) copy-start(bf16[3,1,64,128]{3,2,1,0:T(8,128)(2,1)} %param.14) | copy-start | bytes 147460
  111.2 170.8 %reduce-scatter.8.cloned.1.call-start = ((), (), s32[]{:S(2)}) async-start(), calls=%async_computation.3 | async-start | bytes 1179648 | tf_op jit(solution)/shard_map/reduce_scatter | solution.py:26
  182.8 1.4 collective-permute-start
  211.6 3.3 collective-permute-start.1
  282.9 4.3 %collective-permute-start.2 = (f32[2,64,128]{2,1,0:T(8,128)S(1)}, f32[2,64,128]{2,1,0:T(8,128)S(1)}, u32[]{:S(2)}, u32[]{:S(2)}) collective-permute-start(f32[2,64,128]{2,1,0:T(8,128)S(1)} %select_bitcast_fusion), channel_id=1, source_target_pairs={{0,16},{8,24},{16,0},{24,8},{1,17},{9,25},{17,1},{25,9},{2,18},{10... | collective-permute-start | bytes 196616 | tf_op jit(solution)/shard_map/ppermute | solution.py:10
  288.1 1.3 collective-permute-start.3
  315.6 1.3 collective-permute-start.4
  317.0 8.4 %collective-permute-start.5 = (bf16[2,64,1024]{2,1,0:T(8,128)(2,1)S(1)}, bf16[2,64,1024]{2,1,0:T(8,128)(2,1)S(1)}, u32[]{:S(2)}, u32[]{:S(2)}) collective-permute-start(bf16[2,64,1024]{2,1,0:T(8,128)(2,1)S(1)} %maximum_select_fusion.4), channel_id=1, source_target_pairs={{0,16},{8,24},{16,0},{24,8},{1,17},{9,25},{17,1},{25,9},{2,18},{10... | collective-permute-start | bytes 786440 | tf_op jit(solution)/shard_map/ppermute | solution.py:10
Sparse Core Ops, SparseCore 0:
  15.5 64.7 reduce-scatter.5
  111.3 70.1 all-reduce.2
  219.9 62.0 reduce-scatter.7
where the time goes:
time: 335 us; the launch traced here: 334 us
  waiting for transfers between devices  205 us (61%)
  blocking collectives  78.5 us (23%)
  matrix products  16.7 us (5%)
  between operations  13.3 us (4%)
  local copies, waits for them, and re-layouts  11.3 us (3%)
  other arithmetic  6.65 us (2%)
    reduce_scatter x2, waiting for transfers between devices, collect(): lax.psum_scatter(buffer.reshape(count, members, height, width), 'member',...  123 us
    all_gather x3, blocking collectives, settle(): whole = lax.all_gather(resid, 'member', axis=1, tiled=True)  78.5 us
    unnamed x4, waiting for transfers between devices  69 us
    ppermute x6, waiting for transfers between devices, swapped(): return lax.ppermute(value, axis, pairs)  12.2 us
    dot_general x5, matrix products, spread(): lax.dot_general(onehot, terms.reshape(count, -1), (((0,), (0,)), ((), ())...  9.99 us
  transfers between devices with their start and end apart: 9, of which 7 were waited for; matrix products, arithmetic and copies ran while one was open for 3% of the time, Pallas kernels for 0%

commit v1 on v0

v1 whole, which is shorter than its diff:
```python
import functools

import jax
import jax.numpy as jnp
from jax import lax
from jax.experimental import pallas as pl
from jax.experimental.pallas import tpu as pltpu
from jax.sharding import PartitionSpec as P

MESH = pl.DeviceIdType.MESH
LEVELS = 3


def leaf_kernel(members, rows_ref, values_ref, panels_ref, out_ref, total_ref):
    block = pl.program_id(0)
    terms_each = panels_ref.shape[2]

    @pl.when(block == 0)
    def _():
        total_ref[...] = jnp.zeros_like(total_ref)

    value = values_ref[0]
    for level in range(LEVELS):
        base = members * (2**level - 1)
        for t in range(terms_each):
            term = jnp.dot(value, panels_ref[0, level, t], preferred_element_type=jnp.float32)
            where = base + rows_ref[(block * LEVELS + level) * terms_each + t]
            total_ref[where] = total_ref[where] + term

    @pl.when(block == pl.num_programs(0) - 1)
    def _():
        out_ref[...] = total_ref[...].astype(out_ref.dtype)


def leaf_parts(members, rows, values, panels):
    blocks, levels, terms_each, width, _ = panels.shape
    height = values.shape[1]
    slots = members * (2**LEVELS - 1)
    return pl.pallas_call(
        functools.partial(leaf_kernel, members),
        grid=(blocks,),
        out_shape=jax.ShapeDtypeStruct((slots, height, width), jnp.bfloat16),
        in_specs=[
            pl.BlockSpec(memory_space=pltpu.SMEM),
            pl.BlockSpec((1, height, width), lambda b: (b, 0, 0)),
            pl.BlockSpec((1, levels, terms_each, width, width), lambda b: (b, 0, 0, 0, 0)),
        ],
        out_specs=pl.BlockSpec((slots, height, width), lambda b: (0, 0, 0)),
        scratch_shapes=[pltpu.VMEM((slots, height, width), jnp.float32)],
        name="leaf_parts",
    )(rows.reshape(-1), values, panels)


def solve_kernel(
    members,
    rows_ref,
    leaf_ref,
    sides_ref,
    panels_hbm,
    low_hbm,
    mid_hbm,
    top_hbm,
    out_ref,
    sends,
    parts,
    whole,
    terms,
    panels,
    low,
    mid,
    top,
    local_sem,
    part_send,
    part_recv,
    whole_send,
    whole_recv,
):
    group, member = (lax.axis_index("group"), lax.axis_index("member"))
    inverses = (low, mid, top)
    loads = [
        pltpu.make_async_copy(source, target, local_sem.at[i])
        for i, (source, target) in enumerate(
            ((low_hbm, low), (panels_hbm, panels), (mid_hbm, mid), (top_hbm, top))
        )
    ]

    def place(level):
        count = 2**level
        first_group = group - lax.rem(group, count)
        mine = (group - first_group) * members + member
        return first_group, mine, members * count, members * (count - 1)

    def device(first_group, block):
        return (first_group + lax.div(block, members), lax.rem(block, members))

    def part_copy(level, source, peer, slot):
        first_group, mine, n, base = place(level)
        return pltpu.make_async_remote_copy(
            src_ref=source.at[base + peer],
            dst_ref=parts.at[base + slot],
            send_sem=part_send.at[base + peer],
            recv_sem=part_recv.at[base + slot],
            device_id=device(first_group, peer),
            device_id_type=MESH,
        )

    def whole_copy(level, peer, slot):
        first_group, mine, n, base = place(level)
        return pltpu.make_async_remote_copy(
            src_ref=whole.at[base + mine],
            dst_ref=whole.at[base + slot],
            send_sem=whole_send.at[base + peer],
            recv_sem=whole_recv.at[base + slot],
            device_id=device(first_group, peer),
            device_id_type=MESH,
        )

    def settle(level, source):
        _, mine, n, base = place(level)

        def send(k, _):
            part_copy(level, source, lax.rem(mine + k, n), mine).start()
            return 0

        lax.fori_loop(1, n, send, 0)

        def add(k, total):
            peer = lax.rem(mine + k, n)
            part_copy(level, source, peer, peer).wait_recv()
            return total + parts[base + peer].astype(jnp.float32)

        total = lax.fori_loop(1, n, add, source[base + mine].astype(jnp.float32))
        whole[base + mine] = (sides_ref[level].astype(jnp.float32) - total).astype(jnp.bfloat16)

        def tell(k, _):
            whole_copy(level, lax.rem(mine + k, n), mine).start()
            return 0

        lax.fori_loop(1, n, tell, 0)

        def hear(k, _):
            peer = lax.rem(mine + k, n)
            whole_copy(level, peer, peer).wait_recv()
            return 0

        lax.fori_loop(1, n, hear, 0)
        inverse = inverses[level]
        width = inverse.shape[1]
        chunk = members

        def multiply(i, total):
            start = i * chunk
            pieces = [whole[base + start + c] for c in range(chunk)]
            rows = inverse[pl.ds(pl.multiple_of(start * width, chunk * width), chunk * width), :]
            return total + jnp.dot(
                jnp.concatenate(pieces, axis=1), rows, preferred_element_type=jnp.float32
            )

        total = lax.fori_loop(0, n // chunk, multiply, jnp.zeros(out_ref.shape[1:], jnp.float32))
        value = total.astype(jnp.bfloat16)
        out_ref[level] = value
        return value

    def scatter(level, sources):
        _, mine, n, base = place(level)
        each = rows_ref.shape[1]
        named = [
            (slot * each + t, rows_ref[j, t]) for slot, j in sources for t in range(each)
        ]

        def fill(q, _):
            total = leaf_ref[base + q].astype(jnp.float32)
            for index, row in named:
                total = total + terms[index] * (row == q).astype(jnp.float32)
            sends[base + q] = total.astype(jnp.bfloat16)
            return 0

        lax.fori_loop(0, n, fill, 0)

    def drain(level, source):
        _, mine, n, base = place(level)

        def one(k, _):
            peer = lax.rem(mine + k, n)
            part_copy(level, source, peer, mine).wait_send()
            whole_copy(level, peer, mine).wait_send()
            return 0

        lax.fori_loop(1, n, one, 0)

    def products(value, slot, j):
        each = panels.shape[1]
        for t in range(each):
            terms[slot * each + t] = jnp.dot(
                value, panels[j, t], preferred_element_type=jnp.float32
            )

    for load in loads:
        load.start()
    first_group, mine, n, base = place(LEVELS - 1)
    barrier = pltpu.get_barrier_semaphore()

    def greet(k, _):
        pl.semaphore_signal(
            barrier,
            inc=1,
            device_id=device(first_group, lax.rem(mine + k, n)),
            device_id_type=MESH,
        )
        return 0

    lax.fori_loop(1, n, greet, 0)
    pl.semaphore_wait(barrier, n - 1)
    for load in loads:
        load.wait()

    first = settle(0, leaf_ref)
    products(first, 0, 0)
    products(first, 1, 1)
    scatter(1, [(0, 0)])
    second = settle(1, sends)
    products(second, 2, 2)
    scatter(2, [(1, 1), (2, 2)])
    settle(2, sends)
    drain(0, leaf_ref)
    drain(1, sends)
    drain(2, sends)


def on_device(
    leaf_solution,
    leaf_panels,
    leaf_rows,
    sep_panels,
    sep_rows,
    right_sides,
    inverse_low,
    inverse_mid,
    inverse_top,
):
    members = lax.axis_size("member")
    height, width = (leaf_solution.shape[1], leaf_solution.shape[2])
    slots = members * (2**LEVELS - 1)
    leaf = leaf_parts(members, leaf_rows, leaf_solution, leaf_panels)
    vmem = pl.BlockSpec(memory_space=pltpu.VMEM)
    hbm = pl.BlockSpec(memory_space=pl.ANY)
    each = sep_panels.shape[2]
    out = pl.pallas_call(
        functools.partial(solve_kernel, members),
        out_shape=jax.ShapeDtypeStruct((LEVELS, height, width), jnp.bfloat16),
        in_specs=[pl.BlockSpec(memory_space=pltpu.SMEM), vmem, vmem, hbm, hbm, hbm, hbm],
        out_specs=vmem,
        scratch_shapes=[
            pltpu.VMEM((slots, height, width), jnp.bfloat16),
            pltpu.VMEM((slots, height, width), jnp.bfloat16),
            pltpu.VMEM((slots, height, width), jnp.bfloat16),
            pltpu.VMEM((LEVELS * each, height, width), jnp.float32),
            pltpu.VMEM(sep_panels.shape[1:], jnp.bfloat16),
            pltpu.VMEM(inverse_low.shape[1:], jnp.bfloat16),
            pltpu.VMEM(inverse_mid.shape[1:], jnp.bfloat16),
            pltpu.VMEM(inverse_top.shape[1:], jnp.bfloat16),
            pltpu.SemaphoreType.DMA((4,)),
            pltpu.SemaphoreType.DMA((slots,)),
            pltpu.SemaphoreType.DMA((slots,)),
            pltpu.SemaphoreType.DMA((slots,)),
            pltpu.SemaphoreType.DMA((slots,)),
        ],
        compiler_params=pltpu.CompilerParams(collective_id=0, has_side_effects=True),
        name="solve",
    )(
        sep_rows[0],
        leaf,
        right_sides[:, 0],
        sep_panels[0],
        inverse_low[0],
        inverse_mid[0],
        inverse_top[0],
    )
    return out[:, None]


def solution(mesh):
    placed = (
        P(("group", "member"), None, None),
        P(("group", "member"), None, None, None, None),
        P(("group", "member"), None, None),
        P(("group", "member"), None, None, None, None),
        P(("group", "member"), None, None),
        P(None, ("group", "member"), None, None),
        P(("group", "member"), None, None),
        P(("group", "member"), None, None),
        P(("group", "member"), None, None),
    )
    return jax.shard_map(
        on_device,
        mesh=mesh,
        in_specs=placed,
        out_specs=P(None, ("group", "member"), None, None),
        check_vma=False,
    )
```

time: 335 us -> 74.6 us (0.22)
  waiting for transfers between devices: 205 us -> 0 us
  blocking collectives: 78.5 us -> 0 us
  Pallas kernels: 0 us -> 70.1 us
  matrix products: 16.7 us -> 0 us
  between operations: 13.3 us -> 0.01 us
  local copies, waits for them, and re-layouts: 11.3 us -> 4.11 us
  other arithmetic: 6.65 us -> 0 us
    reduce_scatter x2 -> x0, waiting for transfers between devices: 123 us -> none  [collect(): lax.psum_scatter(buffer.reshape(count, members, height, width), 'member',...]
    all_gather x3 -> x0, blocking collectives: 78.5 us -> none  [settle(): whole = lax.all_gather(resid, 'member', axis=1, tiled=True)]
    pallas_call x0 -> x2, Pallas kernels: none -> 70.1 us  [the longest x1 63.5 us: on_device(): pl.pallas_call(functools.partial(solve_kernel, members), out_shape=jax.Sh...]
    unnamed x4 -> x0, waiting for transfers between devices: 69 us -> none
    dot_general x11 -> x0, matrix products: 16.7 us -> none  [the longest x5 9.99 us: spread(): lax.dot_general(onehot, terms.reshape(count, -1), (((0,), (0,)), ((), ())...]
    ppermute x6 -> x0, waiting for transfers between devices: 12.2 us -> none  [swapped(): return lax.ppermute(value, axis, pairs)]
  transfers between devices with their start and end apart: 9 -> 0, of which waited for: 7 -> 0; matrix products, arithmetic and copies ran while one was open for 3% -> 0% of each run, Pallas kernels for 0% -> 0%
where the time goes in v1:
time: 74.6 us; the launch traced here: 74.2 us
  Pallas kernels  70.1 us (94%)
  local copies, waits for them, and re-layouts  4.11 us (6%)
    pallas_call x1, Pallas kernels, on_device(): pl.pallas_call(functools.partial(solve_kernel, members), out_shape=jax.Sh...  63.5 us
    pallas_call x1, Pallas kernels, leaf_parts(): pl.pallas_call(functools.partial(leaf_kernel, members), grid=(blocks,), o...  6.59 us
    unnamed x3, local copies, waits for them, and re-layouts  3.46 us

profile of v1, /device:TPU:0, one launch (start us, length us, event | category | flops | bytes accessed | tf_op | source)
XLA Modules:
  0.0 74.2 jit_solution(18328416224252248714)
XLA Ops:
  0.0 1.3 %copy.16 = s32[1,3,4]{2,1,0:T(4,128)} copy(s32[1,3,4]{2,0,1:T(1,128)} %param.13) | data formatting | bytes 96
  1.3 0.8 %copy.12 = s32[8,3,4]{2,1,0:T(4,128)S(1)} copy(s32[8,3,4]{0,2,1:T(4,128)} %param.11) | data formatting | bytes 768 | tf_op args[2]
  2.0 0.6 reshape.3.rows_ref
  2.7 6.6 %leaf_parts.1.leaf_ref = bf16[56,64,128]{2,1,0:T(8,128)(2,1)} custom-call(s32[96]{0:T(128)} %reshape.3.rows_ref, bf16[8,64,128]{2,1,0:T(8,128)(2,1)} %values_ref.1, bf16[8,3,4,128,128]{4,3,2,1,0:T(8,128)(2,1)} %panels_ref.1), custom_call_target="tpu_custom_call" | custom-call | tf_op jit(solution)/shard_map/leaf_parts/pallas_call | solution.py:39
  9.3 63.5 %solve.1 = bf16[3,64,128]{2,1,0:T(8,128)(2,1)} custom-call(s32[3,4]{1,0:T(4,128)} %bitcast.17, bf16[56,64,128]{2,1,0:T(8,128)(2,1)} %leaf_parts.1.leaf_ref, bf16[3,64,128]{2,1,0:T(8,128)(2,1)} %bitcast.16, bf16[3,4,128,128]{3,2,1,0:T(8,128)(2,1)} %bitcast.13, bf16[1024,128]{1,0:T(8,128)(2,1)} %bitcast.14, bf16[2048,128]{1,0:T(8,128)(2,1)} %bitcast.12, ...), custom_call_target="tpu_custom_call" | custom-call | tf_op jit(solution)/shard_map/solve/pallas_call | solution.py:248
  72.8 1.4 %copy.18 = bf16[3,1,64,128]{3,2,1,0:T(8,128)(2,1)} copy(bf16[3,1,64,128]{3,2,1,0:T(8,128)(2,1)} %bitcast.15) | data formatting | bytes 98304

commit v2 on v1

v2 whole, which is shorter than its diff:
```python
import functools

import jax
import jax.numpy as jnp
from jax import lax
from jax.experimental import pallas as pl
from jax.experimental.pallas import tpu as pltpu
from jax.sharding import PartitionSpec as P

MESH = pl.DeviceIdType.MESH
LEVELS = 3


def solve_kernel(
    members,
    leaf_rows_ref,
    rows_ref,
    values_ref,
    sides_ref,
    leaf_hbm,
    panels_hbm,
    low_hbm,
    mid_hbm,
    top_hbm,
    out_ref,
    base_sums,
    sends,
    parts,
    whole,
    leaf_terms,
    terms,
    leaf_panels,
    panels,
    low,
    mid,
    top,
    local_sem,
    part_send,
    part_recv,
    whole_send,
    whole_recv,
):
    group, member = (lax.axis_index("group"), lax.axis_index("member"))
    blocks, each = (values_ref.shape[0], panels.shape[1])
    inverses = (low, mid, top)
    pairs = [(leaf_hbm.at[:, level], leaf_panels.at[level]) for level in range(LEVELS)]
    pairs += [(low_hbm, low), (panels_hbm, panels), (mid_hbm, mid), (top_hbm, top)]
    loads = [
        pltpu.make_async_copy(source, target, local_sem.at[i])
        for i, (source, target) in enumerate(pairs)
    ]
    for load in loads:
        load.start()

    def place(level):
        count = 2**level
        first_group = group - lax.rem(group, count)
        mine = (group - first_group) * members + member
        return first_group, mine, members * count, members * (count - 1)

    def device(first_group, block):
        return (first_group + lax.div(block, members), lax.rem(block, members))

    def part_copy(level, peer, slot):
        first_group, mine, n, base = place(level)
        return pltpu.make_async_remote_copy(
            src_ref=sends.at[base + peer],
            dst_ref=parts.at[base + slot],
            send_sem=part_send.at[base + peer],
            recv_sem=part_recv.at[base + slot],
            device_id=device(first_group, peer),
            device_id_type=MESH,
        )

    def whole_copy(level, peer, slot):
        first_group, mine, n, base = place(level)
        return pltpu.make_async_remote_copy(
            src_ref=whole.at[base + mine],
            dst_ref=whole.at[base + slot],
            send_sem=whole_send.at[base + peer],
            recv_sem=whole_recv.at[base + slot],
            device_id=device(first_group, peer),
            device_id_type=MESH,
        )

    def leaf_products(level):
        loads[level].wait()

        def one(b, _):
            value = values_ref[b]
            for t in range(each):
                leaf_terms[b * each + t] = jnp.dot(
                    value, leaf_panels[level, b, t], preferred_element_type=jnp.float32
                )
            return 0

        lax.fori_loop(0, blocks, one, 0)

    def leaf_sum(level, q):
        total = jnp.zeros(out_ref.shape[1:], jnp.float32)
        for b in range(blocks):
            for t in range(each):
                hit = (leaf_rows_ref[level, t, b] == q).astype(jnp.float32)
                total = total + leaf_terms[b * each + t] * hit
        return total

    def term_sum(total, slot, j, q):
        for t in range(each):
            hit = (rows_ref[j, 0, t] == q).astype(jnp.float32)
            total = total + terms[slot * each + t] * hit
        return total

    def products(value, slot, j):
        for t in range(each):
            terms[slot * each + t] = jnp.dot(
                value, panels[j, t], preferred_element_type=jnp.float32
            )

    def leaf_base(level):
        _, mine, n, base = place(level)
        leaf_products(level)

        def one(q, _):
            base_sums[base - members + q] = leaf_sum(level, q)
            return 0

        lax.fori_loop(0, n, one, 0)

    def settle(level, partial, first_filler, second_filler):
        _, mine, n, base = place(level)

        def send(k, _):
            peer = lax.rem(mine + k, n)
            sends[base + peer] = partial(peer).astype(jnp.bfloat16)

            @pl.when(k > 1)
            def _():
                part_copy(level, lax.rem(mine + k - 1, n), mine).start()

            return 0

        lax.fori_loop(1, n, send, 0)
        total = partial(mine)
        part_copy(level, lax.rem(mine + n - 1, n), mine).start()
        first_filler()

        def add(k, total):
            peer = lax.rem(mine + n - k, n)
            part_copy(level, peer, peer).wait_recv()
            return total + parts[base + peer].astype(jnp.float32)

        total = lax.fori_loop(1, n, add, total)
        whole[base + mine] = (sides_ref[level].astype(jnp.float32) - total).astype(jnp.bfloat16)

        def tell(k, _):
            whole_copy(level, lax.rem(mine + k, n), mine).start()
            return 0

        lax.fori_loop(1, n, tell, 0)
        second_filler()
        inverse = inverses[level]
        width = inverse.shape[1]

        def multiply(i, total):
            start = i * members

            def hear(c, _):
                @pl.when(start + c != mine)
                def _():
                    whole_copy(level, start + c, start + c).wait_recv()

                return 0

            lax.fori_loop(0, members, hear, 0)
            pieces = [whole[base + start + c] for c in range(members)]
            at = pl.ds(pl.multiple_of(start * width, members * width), members * width)
            return total + jnp.dot(
                jnp.concatenate(pieces, axis=1), inverse[at, :], preferred_element_type=jnp.float32
            )

        total = lax.fori_loop(0, n // members, multiply, jnp.zeros(out_ref.shape[1:], jnp.float32))
        value = total.astype(jnp.bfloat16)
        out_ref[level] = value
        return value

    def drain(level):
        _, mine, n, base = place(level)

        def one(k, _):
            peer = lax.rem(mine + k, n)
            part_copy(level, peer, mine).wait_send()
            whole_copy(level, peer, mine).wait_send()
            return 0

        lax.fori_loop(1, n, one, 0)

    first_group, mine, n, base = place(LEVELS - 1)
    barrier = pltpu.get_barrier_semaphore()

    def greet(k, _):
        pl.semaphore_signal(
            barrier,
            inc=1,
            device_id=device(first_group, lax.rem(mine + k, n)),
            device_id_type=MESH,
        )
        return 0

    lax.fori_loop(1, n, greet, 0)
    leaf_products(0)
    pl.semaphore_wait(barrier, n - 1)

    def rest():
        leaf_base(2)
        for load in loads[LEVELS:]:
            load.wait()

    def early_top():
        products(first, 1, 1)
        _, mine, n, base = place(2)

        def one(q, _):
            base_sums[base - members + q] = term_sum(base_sums[base - members + q], 1, 1, q)
            return 0

        lax.fori_loop(0, n, one, 0)

    def nothing():
        pass

    first = settle(0, lambda q: leaf_sum(0, q), lambda: leaf_base(1), rest)
    products(first, 0, 0)
    second = settle(1, lambda q: term_sum(base_sums[q], 0, 0, q), early_top, nothing)
    products(second, 2, 2)
    settle(2, lambda q: term_sum(base_sums[2 * members + q], 2, 2, q), nothing, nothing)
    for level in range(LEVELS):
        drain(level)


def on_device(
    leaf_solution,
    leaf_panels,
    leaf_rows,
    sep_panels,
    sep_rows,
    right_sides,
    inverse_low,
    inverse_mid,
    inverse_top,
):
    members = lax.axis_size("member")
    blocks, height, width = leaf_solution.shape
    slots = members * (2**LEVELS - 1)
    vmem = pl.BlockSpec(memory_space=pltpu.VMEM)
    smem = pl.BlockSpec(memory_space=pltpu.SMEM)
    hbm = pl.BlockSpec(memory_space=pl.ANY)
    each = sep_panels.shape[2]
    out = pl.pallas_call(
        functools.partial(solve_kernel, members),
        out_shape=jax.ShapeDtypeStruct((LEVELS, height, width), jnp.bfloat16),
        in_specs=[smem, smem, vmem, vmem, hbm, hbm, hbm, hbm, hbm],
        out_specs=vmem,
        scratch_shapes=[
            pltpu.VMEM((slots - members, height, width), jnp.float32),
            pltpu.VMEM((slots, height, width), jnp.bfloat16),
            pltpu.VMEM((slots, height, width), jnp.bfloat16),
            pltpu.VMEM((slots, height, width), jnp.bfloat16),
            pltpu.VMEM((blocks * each, height, width), jnp.float32),
            pltpu.VMEM((LEVELS * each, height, width), jnp.float32),
            pltpu.VMEM((LEVELS, blocks, each, width, width), jnp.bfloat16),
            pltpu.VMEM(sep_panels.shape[1:], jnp.bfloat16),
            pltpu.VMEM(inverse_low.shape[1:], jnp.bfloat16),
            pltpu.VMEM(inverse_mid.shape[1:], jnp.bfloat16),
            pltpu.VMEM(inverse_top.shape[1:], jnp.bfloat16),
            pltpu.SemaphoreType.DMA((LEVELS + 4,)),
            pltpu.SemaphoreType.DMA((slots,)),
            pltpu.SemaphoreType.DMA((slots,)),
            pltpu.SemaphoreType.DMA((slots,)),
            pltpu.SemaphoreType.DMA((slots,)),
        ],
        compiler_params=pltpu.CompilerParams(collective_id=0, has_side_effects=True),
        name="solve",
    )(
        leaf_rows.transpose(1, 2, 0),
        sep_rows.transpose(1, 0, 2),
        leaf_solution,
        right_sides[:, 0],
        leaf_panels,
        sep_panels[0],
        inverse_low[0],
        inverse_mid[0],
        inverse_top[0],
    )
    return out[:, None]


def solution(mesh):
    placed = (
        P(("group", "member"), None, None),
        P(("group", "member"), None, None, None, None),
        P(("group", "member"), None, None),
        P(("group", "member"), None, None, None, None),
        P(("group", "member"), None, None),
        P(None, ("group", "member"), None, None),
        P(("group", "member"), None, None),
        P(("group", "member"), None, None),
        P(("group", "member"), None, None),
    )
    return jax.shard_map(
        on_device,
        mesh=mesh,
        in_specs=placed,
        out_specs=P(None, ("group", "member"), None, None),
        check_vma=False,
    )
```

time: 74.6 us -> 64.6 us (0.87)
  Pallas kernels: 70.1 us -> 62.9 us
  local copies, waits for them, and re-layouts: 4.11 us -> 1.42 us
    pallas_call x1 -> x0, Pallas kernels: 6.59 us -> none  [leaf_parts(): pl.pallas_call(functools.partial(leaf_kernel, members), grid=(blocks,), o...]
    unnamed x3 -> x1, local copies, waits for them, and re-layouts: 3.46 us -> 1.42 us
where the time goes in v2:
time: 64.6 us; the launch traced here: 64.4 us
  Pallas kernels  62.9 us (97%)
  local copies, waits for them, and re-layouts  1.42 us (2%)
    pallas_call x1, Pallas kernels, on_device(): pl.pallas_call(functools.partial(solve_kernel, members), out_shape=jax.Sh...  62.9 us
    unnamed x1, local copies, waits for them, and re-layouts  1.42 us

profile of v2, /device:TPU:0, one launch (start us, length us, event | category | flops | bytes accessed | tf_op | source)
XLA Modules:
  0.0 64.4 jit_solution(5974070586877512126)
XLA Ops:
  0.0 62.9 %solve.1 = bf16[3,64,128]{2,1,0:T(8,128)(2,1)} custom-call(s32[3,4,8]{2,1,0:T(4,128)} %bitcast.16, s32[3,1,4]{2,1,0:T(1,128)} %bitcast.17, bf16[8,64,128]{2,1,0:T(8,128)(2,1)} %values_ref.1, bf16[3,64,128]{2,1,0:T(8,128)(2,1)} %bitcast.15, bf16[8,3,4,128,128]{4,3,2,1,0:T(8,128)(2,1)} %leaf_hbm.1, bf16[3,4,128,128]{3,2,1,0:T(8,128)(2,1)} %bitcast.12, ...), custom_call_target="tpu_custom_call" | custom-call | tf_op jit(solution)/shard_map/solve/pallas_call | solution.py:258
  63.0 1.4 %copy.12 = bf16[3,1,64,128]{3,2,1,0:T(8,128)(2,1)} copy(bf16[3,1,64,128]{3,2,1,0:T(8,128)(2,1)} %bitcast.14) | data formatting | bytes 98304

commit v3 on v2

--- a/solution.py
+++ b/solution.py
@@ -25,6 +25,7 @@
     out_ref,
     base_sums,
     sends,
+    pair,
     parts,
     whole,
     leaf_terms,
@@ -37,6 +38,9 @@
     local_sem,
     part_send,
     part_recv,
+    pair_send,
+    pair_recv,
+    pass_send,
     whole_send,
     whole_recv,
 ):
@@ -54,32 +58,65 @@
 
     def place(level):
         count = 2**level
+        step = 2 if level > 0 else 1
         first_group = group - lax.rem(group, count)
-        mine = (group - first_group) * members + member
-        return first_group, mine, members * count, members * (count - 1)
-
-    def device(first_group, block):
-        return (first_group + lax.div(block, members), lax.rem(block, members))
+        inside = group - first_group
+        mine = lax.div(inside, step) * members + member
+        size = members * (count // step)
+        return first_group, step, lax.rem(inside, step), mine, size, members * (count - 1)
+
+    def group_of(level, index, side):
+        return lax.div(index, members) * place(level)[1] + side
+
+    def block(level, index, side):
+        return group_of(level, index, side) * members + lax.rem(index, members)
+
+    def device(level, index, side):
+        return (place(level)[0] + group_of(level, index, side), lax.rem(index, members))
 
     def part_copy(level, peer, slot):
-        first_group, mine, n, base = place(level)
+        _, _, side, mine, _, base = place(level)
         return pltpu.make_async_remote_copy(
-            src_ref=sends.at[base + peer],
+            src_ref=sends.at[base + block(level, peer, side)],
             dst_ref=parts.at[base + slot],
             send_sem=part_send.at[base + peer],
             recv_sem=part_recv.at[base + slot],
-            device_id=device(first_group, peer),
+            device_id=device(level, peer, side),
             device_id_type=MESH,
         )
 
-    def whole_copy(level, peer, slot):
-        first_group, mine, n, base = place(level)
+    def pair_copy(level, index):
+        _, _, side, mine, _, base = place(level)
         return pltpu.make_async_remote_copy(
-            src_ref=whole.at[base + mine],
-            dst_ref=whole.at[base + slot],
+            src_ref=sends.at[base + block(level, index, 1 - side)],
+            dst_ref=pair.at[base + index],
+            send_sem=pair_send.at[base + index],
+            recv_sem=pair_recv.at[base + index],
+            device_id=device(level, mine, 1 - side),
+            device_id_type=MESH,
+        )
+
+    def whole_copy(level, peer, origin):
+        _, _, side, mine, _, base = place(level)
+        at = base + block(level, origin, side)
+        return pltpu.make_async_remote_copy(
+            src_ref=whole.at[at],
+            dst_ref=whole.at[at],
             send_sem=whole_send.at[base + peer],
-            recv_sem=whole_recv.at[base + slot],
-            device_id=device(first_group, peer),
+            recv_sem=whole_recv.at[at],
+            device_id=device(level, peer, side),
+            device_id_type=MESH,
+        )
+
+    def pass_copy(level, index, side):
+        _, _, own_side, mine, _, base = place(level)
+        at = base + block(level, index, side)
+        return pltpu.make_async_remote_copy(
+            src_ref=whole.at[at],
+            dst_ref=whole.at[at],
+            send_sem=pass_send.at[base + index],
+            recv_sem=whole_recv.at[at],
+            device_id=device(level, mine, 1 - own_side),
             device_id_type=MESH,
         )
 
@@ -117,7 +154,7 @@
             )
 
     def leaf_base(level):
-        _, mine, n, base = place(level)
+        n, base = (members * 2**level, place(level)[-1])
         leaf_products(level)
 
         def one(q, _):
@@ -127,11 +164,34 @@
         lax.fori_loop(0, n, one, 0)
 
     def settle(level, partial, first_filler, second_filler):
-        _, mine, n, base = place(level)
+        _, step, side, mine, n, base = place(level)
+        paired = step > 1
+        if paired:
+
+            def give(k, _):
+                at = lax.rem(mine + k, n)
+                q = block(level, at, 1 - side)
+                sends[base + q] = partial(q).astype(jnp.bfloat16)
+
+                @pl.when(k > 1)
+                def _():
+                    pair_copy(level, lax.rem(mine + k - 1, n)).start()
+
+                return 0
+
+            lax.fori_loop(1, n + 1, give, 0)
+            pair_copy(level, mine).start()
+
+        def joined(at):
+            total = partial(block(level, at, side))
+            if paired:
+                pair_copy(level, at).wait_recv()
+                total = total + pair[base + at].astype(jnp.float32)
+            return total
 
         def send(k, _):
-            peer = lax.rem(mine + k, n)
-            sends[base + peer] = partial(peer).astype(jnp.bfloat16)
+            at = lax.rem(mine + k, n)
+            sends[base + block(level, at, side)] = joined(at).astype(jnp.bfloat16)
 
             @pl.when(k > 1)
             def _():
@@ -140,8 +200,8 @@
             return 0
 
         lax.fori_loop(1, n, send, 0)
-        total = partial(mine)
         part_copy(level, lax.rem(mine + n - 1, n), mine).start()
+        total = joined(mine)
         first_filler()
 
         def add(k, total):
@@ -150,41 +210,59 @@
             return total + parts[base + peer].astype(jnp.float32)
 
         total = lax.fori_loop(1, n, add, total)
-        whole[base + mine] = (sides_ref[level].astype(jnp.float32) - total).astype(jnp.bfloat16)
+        whole[base + block(level, mine, side)] = (
+            sides_ref[level].astype(jnp.float32) - total
+        ).astype(jnp.bfloat16)
 
         def tell(k, _):
             whole_copy(level, lax.rem(mine + k, n), mine).start()
             return 0
 
         lax.fori_loop(1, n, tell, 0)
+        if paired:
+            pass_copy(level, mine, side).start()
         second_filler()
+
+        def hear(k, _):
+            peer = lax.rem(mine + n - k, n)
+            whole_copy(level, peer, peer).wait_recv()
+            if paired:
+                pass_copy(level, peer, side).start()
+            return 0
+
+        lax.fori_loop(1, n, hear, 0)
         inverse = inverses[level]
         width = inverse.shape[1]
 
-        def multiply(i, total):
-            start = i * members
-
-            def hear(c, _):
-                @pl.when(start + c != mine)
-                def _():
-                    whole_copy(level, start + c, start + c).wait_recv()
-
-                return 0
-
-            lax.fori_loop(0, members, hear, 0)
+        def multiply(i, total, from_side):
+            start = (i * step + from_side) * members
             pieces = [whole[base + start + c] for c in range(members)]
             at = pl.ds(pl.multiple_of(start * width, members * width), members * width)
             return total + jnp.dot(
                 jnp.concatenate(pieces, axis=1), inverse[at, :], preferred_element_type=jnp.float32
             )
 
-        total = lax.fori_loop(0, n // members, multiply, jnp.zeros(out_ref.shape[1:], jnp.float32))
+        total = jnp.zeros(out_ref.shape[1:], jnp.float32)
+        total = lax.fori_loop(
+            0, n // members, lambda i, total: multiply(i, total, side), total
+        )
+        if paired:
+
+            def passed(k, _):
+                peer = lax.rem(mine + n - k, n)
+                pass_copy(level, peer, 1 - side).wait_recv()
+                return 0
+
+            lax.fori_loop(0, n, passed, 0)
+            total = lax.fori_loop(
+                0, n // members, lambda i, total: multiply(i, total, 1 - side), total
+            )
         value = total.astype(jnp.bfloat16)
         out_ref[level] = value
         return value
 
     def drain(level):
-        _, mine, n, base = place(level)
+        _, step, side, mine, n, base = place(level)
 
         def one(k, _):
             peer = lax.rem(mine + k, n)
@@ -193,22 +271,33 @@
             return 0
 
         lax.fori_loop(1, n, one, 0)
-
-    first_group, mine, n, base = place(LEVELS - 1)
+        if step > 1:
+
+            def two(index, _):
+                pair_copy(level, index).wait_send()
+                pass_copy(level, index, side).wait_send()
+                return 0
+
+            lax.fori_loop(0, n, two, 0)
+
+    _, _, side, mine, n, _ = place(LEVELS - 1)
     barrier = pltpu.get_barrier_semaphore()
+    pl.semaphore_signal(
+        barrier, inc=1, device_id=device(LEVELS - 1, mine, 1 - side), device_id_type=MESH
+    )
 
     def greet(k, _):
         pl.semaphore_signal(
             barrier,
             inc=1,
-            device_id=device(first_group, lax.rem(mine + k, n)),
+            device_id=device(LEVELS - 1, lax.rem(mine + k, n), side),
             device_id_type=MESH,
         )
         return 0
 
     lax.fori_loop(1, n, greet, 0)
     leaf_products(0)
-    pl.semaphore_wait(barrier, n - 1)
+    pl.semaphore_wait(barrier, n)
 
     def rest():
         leaf_base(2)
@@ -217,7 +306,7 @@
 
     def early_top():
         products(first, 1, 1)
-        _, mine, n, base = place(2)
+        n, base = (members * 4, place(2)[-1])
 
         def one(q, _):
             base_sums[base - members + q] = term_sum(base_sums[base - members + q], 1, 1, q)
@@ -265,6 +354,7 @@
             pltpu.VMEM((slots, height, width), jnp.bfloat16),
             pltpu.VMEM((slots, height, width), jnp.bfloat16),
             pltpu.VMEM((slots, height, width), jnp.bfloat16),
+            pltpu.VMEM((slots, height, width), jnp.bfloat16),
             pltpu.VMEM((blocks * each, height, width), jnp.float32),
             pltpu.VMEM((LEVELS * each, height, width), jnp.float32),
             pltpu.VMEM((LEVELS, blocks, each, width, width), jnp.bfloat16),
@@ -273,6 +363,9 @@
             pltpu.VMEM(inverse_mid.shape[1:], jnp.bfloat16),
             pltpu.VMEM(inverse_top.shape[1:], jnp.bfloat16),
             pltpu.SemaphoreType.DMA((LEVELS + 4,)),
+            pltpu.SemaphoreType.DMA((slots,)),
+            pltpu.SemaphoreType.DMA((slots,)),
+            pltpu.SemaphoreType.DMA((slots,)),
             pltpu.SemaphoreType.DMA((slots,)),
             pltpu.SemaphoreType.DMA((slots,)),
             pltpu.SemaphoreType.DMA((slots,)),

time: 64.6 us -> 52.6 us (0.81)
  Pallas kernels: 62.9 us -> 50.8 us
    pallas_call x1, Pallas kernels: 62.9 us -> 50.8 us  [on_device(): pl.pallas_call(functools.partial(solve_kernel, members), out_shape=jax.Sh...]
where the time goes in v3:
time: 52.6 us; the launch traced here: 52.2 us
  Pallas kernels  50.8 us (97%)
  local copies, waits for them, and re-layouts  1.42 us (3%)
    pallas_call x1, Pallas kernels, on_device(): pl.pallas_call(functools.partial(solve_kernel, members), out_shape=jax.Sh...  50.8 us
    unnamed x1, local copies, waits for them, and re-layouts  1.42 us

profile of v3, /device:TPU:0, one launch (start us, length us, event | category | flops | bytes accessed | tf_op | source)
XLA Modules:
  0.0 52.2 jit_solution(17607459156852230173)
XLA Ops:
  0.0 50.8 %solve.1 = bf16[3,64,128]{2,1,0:T(8,128)(2,1)} custom-call(s32[3,4,8]{2,1,0:T(4,128)} %bitcast.16, s32[3,1,4]{2,1,0:T(1,128)} %bitcast.17, bf16[8,64,128]{2,1,0:T(8,128)(2,1)} %values_ref.1, bf16[3,64,128]{2,1,0:T(8,128)(2,1)} %bitcast.15, bf16[8,3,4,128,128]{4,3,2,1,0:T(8,128)(2,1)} %leaf_hbm.1, bf16[3,4,128,128]{3,2,1,0:T(8,128)(2,1)} %bitcast.12, ...), custom_call_target="tpu_custom_call" | custom-call | tf_op jit(solution)/shard_map/solve/pallas_call | solution.py:347
  50.8 1.4 %copy.12 = bf16[3,1,64,128]{3,2,1,0:T(8,128)(2,1)} copy(bf16[3,1,64,128]{3,2,1,0:T(8,128)(2,1)} %bitcast.14) | data formatting | bytes 98304

commit v4 on v3

--- a/solution.py
+++ b/solution.py
@@ -53,8 +53,7 @@
         pltpu.make_async_copy(source, target, local_sem.at[i])
         for i, (source, target) in enumerate(pairs)
     ]
-    for load in loads:
-        load.start()
+    loads[0].start()
 
     def place(level):
         count = 2**level
@@ -121,17 +120,12 @@
         )
 
     def leaf_products(level):
-        loads[level].wait()
-
-        def one(b, _):
-            value = values_ref[b]
+        height, width = out_ref.shape[1:]
+        for b in range(blocks):
+            joined = jnp.concatenate([leaf_panels[level, b, t] for t in range(each)], axis=1)
+            product = jnp.dot(values_ref[b], joined, preferred_element_type=jnp.float32)
             for t in range(each):
-                leaf_terms[b * each + t] = jnp.dot(
-                    value, leaf_panels[level, b, t], preferred_element_type=jnp.float32
-                )
-            return 0
-
-        lax.fori_loop(0, blocks, one, 0)
+                leaf_terms[b * each + t] = product[:, t * width : (t + 1) * width]
 
     def leaf_sum(level, q):
         total = jnp.zeros(out_ref.shape[1:], jnp.float32)
@@ -153,12 +147,11 @@
                 value, panels[j, t], preferred_element_type=jnp.float32
             )
 
-    def leaf_base(level):
+    def leaf_base(level, more):
         n, base = (members * 2**level, place(level)[-1])
-        leaf_products(level)
 
         def one(q, _):
-            base_sums[base - members + q] = leaf_sum(level, q)
+            base_sums[base - members + q] = more(leaf_sum(level, q), q)
             return 0
 
         lax.fori_loop(0, n, one, 0)
@@ -191,7 +184,8 @@
 
         def send(k, _):
             at = lax.rem(mine + k, n)
-            sends[base + block(level, at, side)] = joined(at).astype(jnp.bfloat16)
+            if paired:
+                sends[base + block(level, at, side)] = joined(at).astype(jnp.bfloat16)
 
             @pl.when(k > 1)
             def _():
@@ -296,30 +290,38 @@
         return 0
 
     lax.fori_loop(1, n, greet, 0)
+    loads[0].wait()
+    for load in loads[1:]:
+        load.start()
     leaf_products(0)
+
+    def ready(q, _):
+        sends[q] = leaf_sum(0, q).astype(jnp.bfloat16)
+        return 0
+
+    lax.fori_loop(0, members, ready, 0)
     pl.semaphore_wait(barrier, n)
 
-    def rest():
-        leaf_base(2)
-        for load in loads[LEVELS:]:
+    def base_mid():
+        loads[1].wait()
+        leaf_products(1)
+        leaf_base(1, lambda total, q: total)
+
+    def products_top():
+        for load in loads[2:]:
             load.wait()
-
-    def early_top():
+        leaf_products(2)
+
+    def base_top():
         products(first, 1, 1)
-        n, base = (members * 4, place(2)[-1])
-
-        def one(q, _):
-            base_sums[base - members + q] = term_sum(base_sums[base - members + q], 1, 1, q)
-            return 0
-
-        lax.fori_loop(0, n, one, 0)
+        leaf_base(2, lambda total, q: term_sum(total, 1, 1, q))
 
     def nothing():
         pass
 
-    first = settle(0, lambda q: leaf_sum(0, q), lambda: leaf_base(1), rest)
+    first = settle(0, lambda q: leaf_sum(0, q), base_mid, products_top)
     products(first, 0, 0)
-    second = settle(1, lambda q: term_sum(base_sums[q], 0, 0, q), early_top, nothing)
+    second = settle(1, lambda q: term_sum(base_sums[q], 0, 0, q), base_top, nothing)
     products(second, 2, 2)
     settle(2, lambda q: term_sum(base_sums[2 * members + q], 2, 2, q), nothing, nothing)
     for level in range(LEVELS):

time: 52.6 us -> 52.4 us (level)
  no operation moved by 1% of the time
where the time goes in v4:
time: 52.4 us; the launch traced here: 52 us
  Pallas kernels  50.6 us (97%)
  local copies, waits for them, and re-layouts  1.42 us (3%)
    pallas_call x1, Pallas kernels, on_device(): pl.pallas_call(functools.partial(solve_kernel, members), out_shape=jax.Sh...  50.6 us
    unnamed x1, local copies, waits for them, and re-layouts  1.42 us

profile of v4, /device:TPU:0, one launch (start us, length us, event | category | flops | bytes accessed | tf_op | source)
XLA Modules:
  0.0 52.0 jit_solution(9699245325802799079)
XLA Ops:
  0.0 50.6 %solve.1 = bf16[3,64,128]{2,1,0:T(8,128)(2,1)} custom-call(s32[3,4,8]{2,1,0:T(4,128)} %bitcast.16, s32[3,1,4]{2,1,0:T(1,128)} %bitcast.17, bf16[8,64,128]{2,1,0:T(8,128)(2,1)} %values_ref.1, bf16[3,64,128]{2,1,0:T(8,128)(2,1)} %bitcast.15, bf16[8,3,4,128,128]{4,3,2,1,0:T(8,128)(2,1)} %leaf_hbm.1, bf16[3,4,128,128]{3,2,1,0:T(8,128)(2,1)} %bitcast.12, ...), custom_call_target="tpu_custom_call" | custom-call | tf_op jit(solution)/shard_map/solve/pallas_call | solution.py:349
  50.6 1.4 %copy.12 = bf16[3,1,64,128]{3,2,1,0:T(8,128)(2,1)} copy(bf16[3,1,64,128]{3,2,1,0:T(8,128)(2,1)} %bitcast.14) | data formatting | bytes 98304

commit v5 on v4

--- a/solution.py
+++ b/solution.py
@@ -73,6 +73,20 @@
     def device(level, index, side):
         return (place(level)[0] + group_of(level, index, side), lax.rem(index, members))
 
+    def exchange(level, k, hearing=False):
+        _, _, _, mine, n, _ = place(level)
+        if n & (n - 1):
+            return lax.rem(mine + (n - k if hearing else k), n)
+        rows = n // members
+        left = n - k
+        mask = lax.rem(left, rows) * members + lax.div(left, rows)
+        peer = 0
+        bit = 1
+        while bit < n:
+            peer = peer + bit * lax.rem(lax.div(mine, bit) + lax.div(mask, bit), 2)
+            bit *= 2
+        return peer
+
     def part_copy(level, peer, slot):
         _, _, side, mine, _, base = place(level)
         return pltpu.make_async_remote_copy(
@@ -162,13 +176,13 @@
         if paired:
 
             def give(k, _):
-                at = lax.rem(mine + k, n)
+                at = exchange(level, k)
                 q = block(level, at, 1 - side)
                 sends[base + q] = partial(q).astype(jnp.bfloat16)
 
                 @pl.when(k > 1)
                 def _():
-                    pair_copy(level, lax.rem(mine + k - 1, n)).start()
+                    pair_copy(level, exchange(level, k - 1)).start()
 
                 return 0
 
@@ -183,23 +197,23 @@
             return total
 
         def send(k, _):
-            at = lax.rem(mine + k, n)
+            at = exchange(level, k)
             if paired:
                 sends[base + block(level, at, side)] = joined(at).astype(jnp.bfloat16)
 
             @pl.when(k > 1)
             def _():
-                part_copy(level, lax.rem(mine + k - 1, n), mine).start()
+                part_copy(level, exchange(level, k - 1), mine).start()
 
             return 0
 
         lax.fori_loop(1, n, send, 0)
-        part_copy(level, lax.rem(mine + n - 1, n), mine).start()
+        part_copy(level, exchange(level, n - 1), mine).start()
         total = joined(mine)
         first_filler()
 
         def add(k, total):
-            peer = lax.rem(mine + n - k, n)
+            peer = exchange(level, k, True)
             part_copy(level, peer, peer).wait_recv()
             return total + parts[base + peer].astype(jnp.float32)
 
@@ -209,7 +223,7 @@
         ).astype(jnp.bfloat16)
 
         def tell(k, _):
-            whole_copy(level, lax.rem(mine + k, n), mine).start()
+            whole_copy(level, exchange(level, k), mine).start()
             return 0
 
         lax.fori_loop(1, n, tell, 0)
@@ -218,7 +232,7 @@
         second_filler()
 
         def hear(k, _):
-            peer = lax.rem(mine + n - k, n)
+            peer = exchange(level, k, True)
             whole_copy(level, peer, peer).wait_recv()
             if paired:
                 pass_copy(level, peer, side).start()
@@ -243,8 +257,7 @@
         if paired:
 
             def passed(k, _):
-                peer = lax.rem(mine + n - k, n)
-                pass_copy(level, peer, 1 - side).wait_recv()
+                pass_copy(level, k, 1 - side).wait_recv()
                 return 0
 
             lax.fori_loop(0, n, passed, 0)
@@ -259,7 +272,7 @@
         _, step, side, mine, n, base = place(level)
 
         def one(k, _):
-            peer = lax.rem(mine + k, n)
+            peer = exchange(level, k)
             part_copy(level, peer, mine).wait_send()
             whole_copy(level, peer, mine).wait_send()
             return 0
@@ -284,7 +297,7 @@
         pl.semaphore_signal(
             barrier,
             inc=1,
-            device_id=device(LEVELS - 1, lax.rem(mine + k, n), side),
+            device_id=device(LEVELS - 1, exchange(LEVELS - 1, k), side),
             device_id_type=MESH,
         )
         return 0

time: 52.4 us -> 52 us (level)
  no operation moved by 1% of the time
where the time goes in v5:
time: 52 us; the launch traced here: 51.5 us
  Pallas kernels  50.1 us (96%)
  local copies, waits for them, and re-layouts  1.42 us (3%)
    pallas_call x1, Pallas kernels, on_device(): pl.pallas_call(functools.partial(solve_kernel, members), out_shape=jax.Sh...  50.1 us
    unnamed x1, local copies, waits for them, and re-layouts  1.42 us

profile of v5, /device:TPU:0, one launch (start us, length us, event | category | flops | bytes accessed | tf_op | source)
XLA Modules:
  0.0 51.5 jit_solution(17321776607897081914)
XLA Ops:
  0.0 50.1 %solve.1 = bf16[3,64,128]{2,1,0:T(8,128)(2,1)} custom-call(s32[3,4,8]{2,1,0:T(4,128)} %bitcast.16, s32[3,1,4]{2,1,0:T(1,128)} %bitcast.17, bf16[8,64,128]{2,1,0:T(8,128)(2,1)} %values_ref.1, bf16[3,64,128]{2,1,0:T(8,128)(2,1)} %bitcast.15, bf16[8,3,4,128,128]{4,3,2,1,0:T(8,128)(2,1)} %leaf_hbm.1, bf16[3,4,128,128]{3,2,1,0:T(8,128)(2,1)} %bitcast.12, ...), custom_call_target="tpu_custom_call" | custom-call | tf_op jit(solution)/shard_map/solve/pallas_call | solution.py:362
  50.1 1.4 %copy.12 = bf16[3,1,64,128]{3,2,1,0:T(8,128)(2,1)} copy(bf16[3,1,64,128]{3,2,1,0:T(8,128)(2,1)} %bitcast.14) | data formatting | bytes 98304

commit v6 on v5

--- a/solution.py
+++ b/solution.py
@@ -217,7 +217,7 @@
             part_copy(level, peer, peer).wait_recv()
             return total + parts[base + peer].astype(jnp.float32)
 
-        total = lax.fori_loop(1, n, add, total)
+        total = lax.fori_loop(1, n, add, total, unroll=n <= 2 * members)
         whole[base + block(level, mine, side)] = (
             sides_ref[level].astype(jnp.float32) - total
         ).astype(jnp.bfloat16)
@@ -226,7 +226,7 @@
             whole_copy(level, exchange(level, k), mine).start()
             return 0
 
-        lax.fori_loop(1, n, tell, 0)
+        lax.fori_loop(1, n, tell, 0, unroll=n <= 2 * members)
         if paired:
             pass_copy(level, mine, side).start()
         second_filler()
@@ -238,7 +238,7 @@
                 pass_copy(level, peer, side).start()
             return 0
 
-        lax.fori_loop(1, n, hear, 0)
+        lax.fori_loop(1, n, hear, 0, unroll=n <= 2 * members)
         inverse = inverses[level]
         width = inverse.shape[1]
 

time: 52 us -> 51.8 us (level)
  no operation moved by 1% of the time
where the time goes in v6:
time: 51.8 us; the launch traced here: 51.2 us
  Pallas kernels  49.8 us (96%)
  local copies, waits for them, and re-layouts  1.42 us (3%)
    pallas_call x1, Pallas kernels, on_device(): pl.pallas_call(functools.partial(solve_kernel, members), out_shape=jax.Sh...  49.8 us
    unnamed x1, local copies, waits for them, and re-layouts  1.42 us

profile of v6, /device:TPU:0, one launch (start us, length us, event | category | flops | bytes accessed | tf_op | source)
XLA Modules:
  0.0 51.2 jit_solution(10810130986647687487)
XLA Ops:
  0.0 49.8 %solve.1 = bf16[3,64,128]{2,1,0:T(8,128)(2,1)} custom-call(s32[3,4,8]{2,1,0:T(4,128)} %bitcast.16, s32[3,1,4]{2,1,0:T(1,128)} %bitcast.17, bf16[8,64,128]{2,1,0:T(8,128)(2,1)} %values_ref.1, bf16[3,64,128]{2,1,0:T(8,128)(2,1)} %bitcast.15, bf16[8,3,4,128,128]{4,3,2,1,0:T(8,128)(2,1)} %leaf_hbm.1, bf16[3,4,128,128]{3,2,1,0:T(8,128)(2,1)} %bitcast.12, ...), custom_call_target="tpu_custom_call" | custom-call | tf_op jit(solution)/shard_map/solve/pallas_call | solution.py:362
  49.8 1.4 %copy.12 = bf16[3,1,64,128]{3,2,1,0:T(8,128)(2,1)} copy(bf16[3,1,64,128]{3,2,1,0:T(8,128)(2,1)} %bitcast.14) | data formatting | bytes 98304
